TPU v7x, 32 devices: a whole 2x2x4 slice. The times are simulated.
32 devices in a mesh: dp: 4 (over z), tensor: 4 (over y, x), seq: 2 (over core).
Axes of the slice: x: 2, y: 2, z: 4, core: 2. Of those that a mesh axis runs over, the one named last changes fastest.
Arguments:
- hidden: bfloat16 [1024, 4096], P(('dp', 'seq'), 'tensor'), may hold values from -6 to 6
- w_in: bfloat16 [4096, 512], P('tensor'), may hold values from -0.09375 to 0.09375
- embed: bfloat16 [1024, 512], replicated, may hold values from -16 to 16
- gain: float32 [512], replicated, may hold values from 0.1 to 1.9
- w_head: bfloat16 [512, 1024], replicated, may hold values from -2 to 2
- tokens: int32 [1024, 8], P(('dp', 'seq')), may hold values from 0 to 1023
- frame_mask: int32 [1024], P(('dp', 'seq')), may hold values from 0 to 1, as said below
Outputs:
- loss: float32 [], replicated
- grad_head: float32 [524288], P(('dp', 'tensor', 'seq'))
- grad_hidden: bfloat16 [1024, 4096], P(('dp', 'seq'), 'tensor')
Inputs may be any that keep to these rules, and one draw needn't show every extreme that they name: `frame_mask`: frame 0 always counts.
All inputs are finite; a program needn't handle non-finite values.
Results may differ from a plain program's by a relative error of at most 0.015.
Values may be sent and summed in bfloat16 or wider, within the bound.
A program may use at most 64 MiB of HBM per device.

v0:
```python
import jax
import jax.numpy as jnp
from jax import lax
from jax.sharding import PartitionSpec as P


def decode_terms(context, tok_rows, mask_rows, embed, gain, w_head, count_fn):
    frames = context.shape[0]
    width = context.shape[1]
    steps = tok_rows.shape[1]
    before = embed[tok_rows[:, :-1]].astype(jnp.float32)
    leading = jnp.zeros((frames, 1, width), jnp.float32)
    inputs = context.astype(jnp.float32)[:, None, :] + jnp.concatenate([leading, before], 1)
    inverse = lax.rsqrt(jnp.mean(inputs * inputs, -1, keepdims=True) + 1e-06)
    normed = inputs * inverse
    scaled = (normed * gain).astype(jnp.bfloat16)
    flat = scaled.reshape(frames * steps, width)
    logits = jnp.dot(flat, w_head, preferred_element_type=jnp.float32)
    top = jnp.max(logits, -1, keepdims=True)
    total = top[:, 0] + jnp.log(jnp.sum(jnp.exp(logits - top), -1))
    target = tok_rows.reshape(-1)
    onehot = (target[:, None] == jnp.arange(w_head.shape[1], dtype=jnp.int32)[None, :]).astype(
        jnp.float32
    )
    nll = total - jnp.sum(logits * onehot, -1)
    weights = (mask_rows.astype(jnp.float32)[:, None] * jnp.ones((1, steps), jnp.float32)).reshape(
        -1
    )
    count, loss_sum = count_fn(
        steps * jnp.sum(mask_rows.astype(jnp.float32)), jnp.sum(weights * nll)
    )
    probs = jnp.exp(logits - total[:, None])
    grad_logits = ((probs - onehot) * weights[:, None] / count).astype(jnp.bfloat16)
    head_term = lax.dot_general(
        flat, grad_logits, (((0,), (0,)), ((), ())), preferred_element_type=jnp.float32
    )
    grad_scaled = lax.dot_general(
        grad_logits, w_head, (((1,), (1,)), ((), ())), preferred_element_type=jnp.float32
    )
    scaled_grad = grad_scaled.reshape(inputs.shape) * gain
    grad_inputs = inverse * (
        scaled_grad - normed * jnp.mean(scaled_grad * normed, -1, keepdims=True)
    )
    grad_context = jnp.sum(grad_inputs, 1).astype(jnp.bfloat16)
    return (loss_sum / count, head_term, grad_context)


def add_totals(count_local, loss_local):
    return lax.psum((count_local, loss_local), ("dp", "tensor", "seq"))


def per_device(hidden, w_in, embed, gain, w_head, tokens, frame_mask):
    groups = lax.axis_size("tensor")
    rows = hidden.shape[0] // groups
    context = lax.psum_scatter(
        jnp.dot(hidden, w_in, preferred_element_type=jnp.float32),
        "tensor",
        scatter_dimension=0,
        tiled=True,
    ).astype(jnp.bfloat16)
    offset = lax.axis_index("tensor") * rows
    tok_rows = lax.dynamic_slice_in_dim(tokens, offset, rows, 0)
    mask_rows = lax.dynamic_slice_in_dim(frame_mask, offset, rows, 0)
    loss, head_term, grad_context = decode_terms(
        context, tok_rows, mask_rows, embed, gain, w_head, add_totals
    )
    flat_term = head_term.reshape(-1)
    partial_grad = lax.psum_scatter(
        flat_term.astype(jnp.bfloat16), "dp", scatter_dimension=0, tiled=True
    ).astype(jnp.float32)
    grad_head = lax.psum_scatter(partial_grad, ("tensor", "seq"), scatter_dimension=0, tiled=True)
    product = lax.dot_general(
        lax.all_gather(grad_context, "tensor", axis=0, tiled=True),
        w_in,
        (((1,), (1,)), ((), ())),
        preferred_element_type=jnp.float32,
    )
    grad_hidden = product.astype(jnp.bfloat16)
    return (loss, grad_head, grad_hidden)


def solution(mesh):
    placed = (
        P(("dp", "seq"), "tensor"),
        P("tensor", None),
        P(),
        P(),
        P(),
        P(("dp", "seq"), None),
        P(("dp", "seq")),
    )
    return jax.shard_map(
        per_device,
        mesh=mesh,
        in_specs=placed,
        out_specs=(P(), P(("dp", "tensor", "seq")), P(("dp", "seq"), "tensor")),
        check_vma=False,
    )
```

profile of v0, /device:TPU:0, one launch (start us, length us, event | category | flops | bytes accessed | tf_op | source)
XLA Modules:
  0.0 203.0 jit_solution(7871489259881048414)
XLA Ops:
  7.2 0.0 copy-start
  7.2 0.0 copy-start.4
  7.2 0.0 copy-start.1
  7.2 0.0 reduce-scatter.2.cloned.1.call-start
  7.2 2.5 %fusion.11 = f32[128,512]{1,0:T(8,128)} fusion(bf16[128,1024]{1,0:T(8,128)(2,1)} %param.7, bf16[1024,512]{1,0:T(8,128)(2,1)} %param.8), kind=kOutput, calls=%fused_computation.32 | convolution fusion | flops 134217728 | bytes 1572864 | tf_op jit(solution)/shard_map/dot_general | solution.py:56
  9.7 0.0 reduce-scatter.2.cloned.1.call-update
  9.7 0.0 all-reduce.7.cloned.1.call-start
  9.8 0.0 copy-done.4
  9.8 0.1 constant_dynamic-slice_fusion
  9.9 0.1 copy.13
  9.9 0.1 copy.12
  10.0 0.1 reshape.51
  10.2 0.0 copy-done.1
  10.2 0.0 copy-start.5
  10.2 1.1 gather_fusion
  11.3 0.0 copy-start.3
  11.3 0.1 reshape.50
  11.4 0.1 eq.15
  11.4 0.0 copy-done.5
  11.5 0.7 fusion.9
  12.1 0.1 mul.71
  12.2 0.1 mul.72
  13.0 25.5 %reduce-scatter.2.cloned.1.call-done = f32[32,512]{1,0:T(8,128)} async-done(((f32[128,512]{1,0:T(8,128)}), f32[32,512]{1,0:T(8,128)}) %reduce-scatter.2.cloned.1.call-update) | async-done | bytes 65552 | tf_op jit(solution)/shard_map/reduce_scatter | solution.py:55
  38.4 0.8 convert_convert_fusion
  39.3 0.2 multiply_reduce_fusion.2
  39.5 0.0 copy-done
  39.5 0.0 copy-done.3
  39.5 0.6 fusion.10
  40.1 0.5 select_reduce_fusion
  40.6 0.6 multiply_reduce_fusion.3
  41.2 39.5 %all-reduce.3 = (f32[]{:T(128)}, f32[]{:T(128)}) all-reduce(f32[]{:T(128)} %get-tuple-element.9, f32[]{:T(128)S(6)} %mul_shard_map.3), channel_id=1, replica_groups=mesh['dp'=4,'tensor'=4,'seq'=2] {'dp','tensor','seq'}, use_global_device_ids=true, to_apply=%region_6.0 | all-reduce | flops 2 | bytes 16 | tf_op jit(solution)/shard_map/psum | solution.py:49
  80.6 1.1 divide_convert_fusion
  81.7 0.6 fusion
  82.3 1.3 copy.14
  83.6 0.0 all-reduce.7.cloned.1.call-update
  83.6 0.0 all-reduce.9.cloned.1.call-start
  83.7 0.6 copy-done.7
  84.3 0.6 dynamic-slice
  84.9 0.6 dynamic-slice.2
  86.7 0.6 multiply_reduce_fusion.1
  87.3 0.3 multiply_reduce_fusion
  87.7 49.0 %all-reduce.7.cloned.1.call-done = bf16[524288]{0:T(1024)(128)(2,1)} async-done(((bf16[524288]{0:T(1024)(128)(2,1)}), bf16[524288]{0:T(1024)(128)(2,1)}) %all-reduce.7.cloned.1.call-update) | async-done | bytes 1048592
  136.6 1.8 dynamic-slice_convert_fusion
  138.4 0.0 all-reduce.9.cloned.1.call-update
  138.5 8.9 %all_gather.3 = bf16[128,512]{1,0:T(8,128)(2,1)S(1)} all-gather(bf16[32,512]{1,0:T(8,128)(2,1)S(1)} %multiply_reduce_fusion), channel_id=1, replica_groups=mesh['dp'=4,'tensor'=4,'seq'=2] {'tensor'}, dimensions={0}, use_global_device_ids=true | all-gather | bytes 163840 | tf_op jit(solution)/shard_map/all_gather | solution.py:73
  148.7 1.2 convolution_convert_fusion.1
  149.9 43.9 %all-reduce.9.cloned.1.call-done = f32[131072]{0:T(1024)} async-done(((f32[131072]{0:T(1024)}), f32[131072]{0:T(1024)}) %all-reduce.9.cloned.1.call-update) | async-done | bytes 524304
  193.8 1.5 dynamic-slice.3
  (9 shorter events, 0.0 us)
Async XLA Ops:
  7.2 32.3 %copy-start = (bf16[512,1024]{1,0:T(8,128)(2,1)S(1)}, bf16[512,1024]{1,0:T(8,128)(2,1)}, u32[]{:S(2)}) copy-start(bf16[512,1024]{1,0:T(8,128)(2,1)} %param.11) | copy-start | bytes 3145732
  7.2 2.6 %copy-start.4 = (s32[128,8]{0,1:T(8,128)S(1)}, s32[128,8]{0,1:T(8,128)}, u32[]{:S(2)}) copy-start(s32[128,8]{0,1:T(8,128)} %param.12) | copy-start | bytes 12292
  7.2 3.0 %copy-start.1 = (bf16[1024,512]{1,0:T(8,128)(2,1)S(1)}, bf16[1024,512]{1,0:T(8,128)(2,1)}, u32[]{:S(2)}) copy-start(bf16[1024,512]{1,0:T(8,128)(2,1)} %param.9) | copy-start | bytes 3145732
  7.2 31.2 %reduce-scatter.2.cloned.1.call-start = ((), (), s32[]{:S(2)}) async-start(), calls=%async_computation.1 | async-start | bytes 327680 | tf_op jit(solution)/shard_map/reduce_scatter | solution.py:55
  9.7 126.9 %all-reduce.7.cloned.1.call-start = ((), (), s32[]{:S(2)}) async-start(), calls=%async_computation.2 | async-start | bytes 2097152
  10.2 1.3 copy-start.5
  11.3 28.2 %copy-start.3 = (f32[512]{0:T(512)S(1)}, f32[512]{0:T(512)}, u32[]{:S(2)}) copy-start(f32[512]{0:T(512)} %param.10) | copy-start | bytes 6148
  83.6 0.7 copy-start.7
  83.6 1.2 copy-start.6
  83.6 110.2 %all-reduce.9.cloned.1.call-start = ((), (), s32[]{:S(2)}) async-start(), calls=%async_computation.3 | async-start | bytes 1048576
  87.3 61.4 %copy-start.2 = (bf16[1024,512]{1,0:T(8,128)(2,1)S(1)}, bf16[1024,512]{1,0:T(8,128)(2,1)}, u32[]{:S(2)}) copy-start(bf16[1024,512]{1,0:T(8,128)(2,1)} %param.8) | copy-start | bytes 3145732
Sparse Core Ops, SparseCore 0:
  11.3 27.0 reduce-scatter.1
  83.8 52.8 all-reduce.6
  139.7 54.0 all-reduce.8
where the time goes:
time: 203 us
  waiting for transfers between devices  118 us (58%)
  blocking collectives  48.4 us (24%)
  between operations  18.3 us (9%)
  local copies, waits for them, and re-layouts  6.32 us (3%)
  other arithmetic  6.03 us (3%)
  matrix products  5.43 us (3%)
    unnamed x5, waiting for transfers between devices  92.9 us
    psum x1, blocking collectives, add_totals(): return lax.psum((count_local, loss_local), ('dp', 'tensor', 'seq'))  39.5 us
    reduce_scatter x1, waiting for transfers between devices, per_device(): lax.psum_scatter(jnp.dot(hidden, w_in, preferred_element_type=jnp.float32...  25.5 us
    all_gather x1, blocking collectives, per_device(): lax.all_gather(grad_context, 'tensor', axis=0, tiled=True)  8.89 us
    unnamed x20, local copies, waits for them, and re-layouts  4.57 us
  transfers between devices with their start and end apart: 3, of which 3 were waited for; matrix products, arithmetic and copies ran while one was open for 3% of the time, Pallas kernels for 0%

commit v1 on v0

--- a/solution.py
+++ b/solution.py
@@ -1,7 +1,15 @@
+import functools
+
 import jax
 import jax.numpy as jnp
 from jax import lax
+from jax.experimental import pallas as pl
+from jax.experimental.pallas import tpu as pltpu
 from jax.sharding import PartitionSpec as P
+
+F32 = jnp.float32
+BF16 = jnp.bfloat16
+MESH = pl.DeviceIdType.MESH
 
 
 def decode_terms(context, tok_rows, mask_rows, embed, gain, w_head, count_fn):
@@ -49,7 +57,7 @@
     return lax.psum((count_local, loss_local), ("dp", "tensor", "seq"))
 
 
-def per_device(hidden, w_in, embed, gain, w_head, tokens, frame_mask):
+def per_device_plain(hidden, w_in, embed, gain, w_head, tokens, frame_mask):
     groups = lax.axis_size("tensor")
     rows = hidden.shape[0] // groups
     context = lax.psum_scatter(
@@ -79,7 +87,305 @@
     return (loss, grad_head, grad_hidden)
 
 
+def kernel(
+    sizes, hidden_h, w_in_h, embed_h, gain_h, w_head_h, tokens_h, mask_h,
+    loss_o, head_o, gh_o,
+    hidden, w_in, embed, gain, w_head, tokens, mask,
+    ctx_own, ctx_send, ctx_recv, cnt, cnt_recv, gath, scaled, gl, hs, r1, s1, r2, s2, r3,
+    gc, gh, ls1, ls1_r, ls2, ls2_r, ls3, ls3_r,
+    in_sem, out_sem, ctx_ss, ctx_rs, cnt_ss, cnt_rs, gc_ss, gc_rs,
+    h1_ss, h1_rs, h2_ss, h2_rs, h3_ss, h3_rs, l_ss, l_rs,
+):
+    DP, T, S = sizes
+    a, t, s = lax.axis_index("dp"), lax.axis_index("tensor"), lax.axis_index("seq")
+    steps, nframes = tokens.shape
+    frames = nframes // T
+    width, vocab = w_head.shape
+    rows = frames * steps
+    piece = width // (DP * T * S)
+
+    barrier = pltpu.get_barrier_semaphore()
+    peers_t = [{"tensor": lax.rem(t + d, T)} for d in range(1, T)]
+    peers_g = [
+        {"dp": lax.rem(a + d, DP), "seq": lax.rem(s + e, S)}
+        for d in range(DP)
+        for e in range(S)
+        if d or e
+    ]
+    for peer in peers_t + peers_g:
+        pl.semaphore_signal(barrier, inc=1, device_id=peer, device_id_type=MESH)
+
+    loads = [
+        pltpu.make_async_copy(src, dst, in_sem.at[i])
+        for i, (src, dst) in enumerate(
+            [
+                (hidden_h, hidden),
+                (w_in_h, w_in),
+                (mask_h, mask),
+                (tokens_h, tokens),
+                (embed_h, embed),
+                (gain_h, gain),
+                (w_head_h, w_head),
+            ]
+        )
+    ]
+    for load in loads:
+        load.start()
+
+    sends = []
+
+    def send(src, dst, ss, rs, peer):
+        copy = pltpu.make_async_remote_copy(
+            src_ref=src, dst_ref=dst, send_sem=ss, recv_sem=rs, device_id=peer, device_id_type=MESH
+        )
+        copy.start()
+        sends.append(copy)
+        return copy
+
+    loads[0].wait()
+    loads[1].wait()
+    part = jnp.dot(hidden[...], w_in[...], preferred_element_type=F32).reshape(T, frames, width)
+    ctx_send[...] = part.astype(BF16)
+    ctx_own[...] = part
+    loads[2].wait()
+    mask_row = mask[...].astype(F32)
+    cnt[...] = jnp.zeros(cnt.shape, F32) + jnp.sum(mask_row)
+    pl.semaphore_wait(barrier, len(peers_t) + len(peers_g))
+    ctx_copies = [
+        send(ctx_send.at[lax.rem(t + d, T)], ctx_recv.at[d - 1], ctx_ss.at[d - 1], ctx_rs.at[d - 1],
+             peers_t[d - 1])
+        for d in range(1, T)
+    ]
+    cnt_copies = [
+        send(cnt, cnt_recv.at[i], cnt_ss.at[i], cnt_rs.at[i], peer) for i, peer in enumerate(peers_g)
+    ]
+
+    loads[3].wait()
+    spot = lax.broadcasted_iota(jnp.int32, (frames, nframes), 0) + t * frames
+    here = lax.broadcasted_iota(jnp.int32, (frames, nframes), 1)
+    mine = spot == here
+    tok = tokens[...].astype(F32)
+    lanes = lax.broadcasted_iota(jnp.int32, (frames, vocab), 1).astype(F32)
+    hot = [
+        jnp.sum(jnp.where(mine, tok[k : k + 1, :], 0.0), 1, keepdims=True) == lanes
+        for k in range(steps)
+    ]
+    loads[4].wait()
+    prev = jnp.concatenate([jnp.where(h, 1.0, 0.0).astype(BF16) for h in hot[:-1]], 0)
+    gath[...] = jnp.dot(prev, embed[...], preferred_element_type=F32)
+    mcol = jnp.sum(jnp.where(mine, mask_row, 0.0), 1, keepdims=True)
+    loads[5].wait()
+    loads[6].wait()
+    gvec = gain[...]
+
+    ctx = ctx_own[t]
+    for d in range(1, T):
+        ctx_copies[d - 1].wait_recv()
+        ctx = ctx + ctx_recv[d - 1].astype(F32)
+    ctx = ctx.astype(BF16).astype(F32)
+    inputs = jnp.concatenate([ctx] * steps, 0) + jnp.concatenate(
+        [jnp.zeros((frames, width), F32), gath[...]], 0
+    )
+    inverse = lax.rsqrt(jnp.mean(inputs * inputs, -1, keepdims=True) + 1e-06)
+    normed = inputs * inverse
+    flat = (normed * gvec).astype(BF16)
+    scaled[...] = flat
+    logits = jnp.dot(flat, w_head[...], preferred_element_type=F32)
+    top = jnp.max(logits, -1, keepdims=True)
+    powers = jnp.exp(logits - top)
+    norm = jnp.sum(powers, -1, keepdims=True)
+    total = top + jnp.log(norm)
+    onehot = jnp.concatenate([jnp.where(h, 1.0, 0.0) for h in hot], 0)
+    weights = jnp.concatenate([mcol] * steps, 0)
+    nll = total - jnp.sum(logits * onehot, -1, keepdims=True)
+    grads = ((powers * (1.0 / norm) - onehot) * weights).astype(BF16)
+    gl[...] = grads
+
+    chunk = width // DP
+    order = [lax.rem(a + 1 + j, DP) for j in range(DP)]
+    h1 = []
+    for j in range(DP):
+        c = order[j]
+        cols = scaled[:, pl.ds(pl.multiple_of(c * chunk, chunk), chunk)]
+        term = lax.dot_general(
+            cols, gl[...], (((0,), (0,)), ((), ())), preferred_element_type=F32
+        )
+        hs[j] = term.astype(BF16).reshape(T, S, piece, vocab)
+        for e in range(1, S):
+            h1.append(
+                send(hs.at[j, :, lax.rem(s + e, S)], r1.at[j, e - 1], h1_ss.at[j, e - 1],
+                     h1_rs.at[j, e - 1], {"seq": lax.rem(s + e, S)})
+            )
+    ls1[...] = jnp.zeros(ls1.shape, F32) + jnp.sum(weights * nll)
+    n = 0
+    lc1 = []
+    for e in range(1, S):
+        lc1.append(send(ls1, ls1_r.at[e - 1], l_ss.at[n], l_rs.at[n], {"seq": lax.rem(s + e, S)}))
+        n += 1
+
+    grad_scaled = lax.dot_general(
+        gl[...], w_head[...], (((1,), (1,)), ((), ())), preferred_element_type=F32
+    )
+    g = grad_scaled * gvec
+    gi = inverse * (g - normed * jnp.mean(g * normed, -1, keepdims=True))
+    gsum = gi[0:frames]
+    for k in range(1, steps):
+        gsum = gsum + gi[k * frames : (k + 1) * frames]
+    gc[t] = gsum.astype(BF16)
+    gc_copies = [
+        send(gc.at[t], gc.at[t], gc_ss.at[d - 1], gc_rs.at[d - 1], peers_t[d - 1])
+        for d in range(1, T)
+    ]
+
+    h2 = []
+    for j in range(DP):
+        acc = hs[j, :, s].astype(F32)
+        for e in range(1, S):
+            h1[j * (S - 1) + e - 1].wait_recv()
+            acc = acc + r1[j, e - 1].astype(F32)
+        s1[j] = acc.astype(BF16)
+        for d in range(1, T):
+            h2.append(
+                send(s1.at[j, lax.rem(t + d, T)], r2.at[j, d - 1], h2_ss.at[j, d - 1],
+                     h2_rs.at[j, d - 1], peers_t[d - 1])
+            )
+    lsum = ls1[...]
+    for e in range(1, S):
+        lc1[e - 1].wait_recv()
+        lsum = lsum + ls1_r[e - 1]
+    ls2[...] = lsum
+    lc2 = []
+    for d in range(1, T):
+        lc2.append(send(ls2, ls2_r.at[d - 1], l_ss.at[n], l_rs.at[n], peers_t[d - 1]))
+        n += 1
+
+    total_mask = cnt[...]
+    for i in range(len(peers_g)):
+        cnt_copies[i].wait_recv()
+        total_mask = total_mask + cnt_recv[i]
+    share = 1.0 / (total_mask[0:1, 0:1] * steps)
+    for d in range(1, T):
+        gc_copies[d - 1].wait_recv()
+    product = lax.dot_general(
+        gc[...].reshape(nframes, width), w_in[...], (((1,), (1,)), ((), ())),
+        preferred_element_type=F32,
+    )
+    gh[...] = (product * share).astype(BF16)
+    out_copy = pltpu.make_async_copy(gh, gh_o, out_sem)
+    out_copy.start()
+
+    h3 = []
+    for j in range(DP):
+        acc = s1[j, t].astype(F32)
+        for d in range(1, T):
+            h2[j * (T - 1) + d - 1].wait_recv()
+            acc = acc + r2[j, d - 1].astype(F32)
+        if j < DP - 1:
+            s2[j] = acc.astype(BF16)
+            h3.append(
+                send(s2.at[j], r3.at[j], h3_ss.at[j], h3_rs.at[j], {"dp": order[j]})
+            )
+    lsum = ls2[...]
+    for d in range(1, T):
+        lc2[d - 1].wait_recv()
+        lsum = lsum + ls2_r[d - 1]
+    ls3[...] = lsum
+    lc3 = []
+    for d in range(1, DP):
+        lc3.append(
+            send(ls3, ls3_r.at[d - 1], l_ss.at[n], l_rs.at[n], {"dp": lax.rem(a + d, DP)})
+        )
+        n += 1
+    for j in range(DP - 1):
+        h3[j].wait_recv()
+        acc = acc + r3[j].astype(F32)
+    acc = acc * share
+    groups = vocab // 128
+    for b in range(groups):
+        head_o[pl.ds(b, piece, stride=groups), :] = acc[:, b * 128 : (b + 1) * 128]
+    for d in range(1, DP):
+        lc3[d - 1].wait_recv()
+        lsum = lsum + ls3_r[d - 1]
+    loss_o[...] = lsum[0:1, 0:1] * share
+    out_copy.wait()
+    for copy in sends:
+        copy.wait_send()
+
+
+def per_device_kernel(hidden, w_in, embed, gain, w_head, tokens, frame_mask):
+    DP, T, S = lax.axis_size("dp"), lax.axis_size("tensor"), lax.axis_size("seq")
+    nframes, feats = hidden.shape
+    steps = tokens.shape[1]
+    frames = nframes // T
+    width, vocab = w_head.shape
+    rows = frames * steps
+    piece = width // (DP * T * S)
+    G = DP * S - 1
+    V = pltpu.VMEM
+    dma = pltpu.SemaphoreType.DMA
+    scratch = [
+        V(hidden.shape, BF16), V(w_in.shape, BF16), V(embed.shape, BF16), V((1, width), F32),
+        V(w_head.shape, BF16), V((steps, nframes), jnp.int32), V((1, nframes), jnp.int32),
+        V((T, frames, width), F32),
+        V((T, frames, width), BF16),
+        V((T - 1, frames, width), BF16),
+        V((8, 128), F32),
+        V((G, 8, 128), F32),
+        V((rows - frames, width), F32),
+        V((rows, width), BF16),
+        V((rows, vocab), BF16),
+        V((DP, T, S, piece, vocab), BF16),
+        V((DP, S - 1, T, piece, vocab), BF16),
+        V((DP, T, piece, vocab), BF16),
+        V((DP, T - 1, piece, vocab), BF16),
+        V((DP - 1, piece, vocab), BF16),
+        V((DP - 1, piece, vocab), BF16),
+        V((T, frames, width), BF16),
+        V((nframes, feats), BF16),
+        V((8, 128), F32), V((S - 1, 8, 128), F32),
+        V((8, 128), F32), V((T - 1, 8, 128), F32),
+        V((8, 128), F32), V((DP - 1, 8, 128), F32),
+        dma((7,)), dma,
+        dma((T - 1,)), dma((T - 1,)), dma((G,)), dma((G,)), dma((T - 1,)), dma((T - 1,)),
+        dma((DP, S - 1)), dma((DP, S - 1)), dma((DP, T - 1)), dma((DP, T - 1)),
+        dma((DP - 1,)), dma((DP - 1,)), dma((S + T + DP - 3,)), dma((S + T + DP - 3,)),
+    ]
+    loss, head, grad_hidden = pl.pallas_call(
+        functools.partial(kernel, (DP, T, S)),
+        out_shape=(
+            jax.ShapeDtypeStruct((1, 1), F32),
+            jax.ShapeDtypeStruct((piece * vocab // 128, 128), F32),
+            jax.ShapeDtypeStruct((nframes, feats), BF16),
+        ),
+        in_specs=[pl.BlockSpec(memory_space=pl.ANY)] * 7,
+        out_specs=(
+            pl.BlockSpec(memory_space=pltpu.VMEM),
+            pl.BlockSpec(memory_space=pltpu.VMEM),
+            pl.BlockSpec(memory_space=pl.ANY),
+        ),
+        scratch_shapes=scratch,
+        compiler_params=pltpu.CompilerParams(
+            collective_id=0, has_side_effects=True, vmem_limit_bytes=63 << 20
+        ),
+        name="decode",
+    )(hidden, w_in, embed, gain.reshape(1, -1), w_head, tokens.T, frame_mask.reshape(1, -1))
+    return loss.reshape(()), head.reshape(-1), grad_hidden
+
+
 def solution(mesh):
+    def per_device(hidden, w_in, embed, gain, w_head, tokens, frame_mask):
+        DP, T, S = mesh.shape["dp"], mesh.shape["tensor"], mesh.shape["seq"]
+        width, vocab = w_head.shape
+        fits = (
+            width % (16 * DP * T * S) == 0
+            and width % (128 * DP) == 0
+            and vocab % 128 == 0
+            and hidden.shape[0] % (16 * T) == 0
+            and min(DP, T, S) > 1
+        )
+        run = per_device_kernel if fits else per_device_plain
+        return run(hidden, w_in, embed, gain, w_head, tokens, frame_mask)
+
     placed = (
         P(("dp", "seq"), "tensor"),
         P("tensor", None),

time: 203 us -> 31.1 us (0.15)
  waiting for transfers between devices: 118 us -> 0 us
  blocking collectives: 48.4 us -> 0 us
  Pallas kernels: 0 us -> 25.5 us
  between operations: 18.3 us -> 2.33 us
  other arithmetic: 6.03 us -> 0 us
  matrix products: 5.43 us -> 0 us
  local copies, waits for them, and re-layouts: 6.32 us -> 3.14 us
    unnamed x5 -> x0, waiting for transfers between devices: 92.9 us -> none
    psum x1 -> x0, blocking collectives: 39.5 us -> none  [add_totals(): return lax.psum((count_local, loss_local), ('dp', 'tensor', 'seq'))]
    reduce_scatter x1 -> x0, waiting for transfers between devices: 25.5 us -> none  [per_device(): lax.psum_scatter(jnp.dot(hidden, w_in, preferred_element_type=jnp.float32...]
    pallas_call x0 -> x1, Pallas kernels: none -> 25.5 us  [per_device_kernel(): pl.pallas_call(functools.partial(kernel, (DP, T, S)), out_shape=(jax.Shap...]
    all_gather x1 -> x0, blocking collectives: 8.89 us -> none  [per_device(): lax.all_gather(grad_context, 'tensor', axis=0, tiled=True)]
    dot_general x5 -> x0, matrix products: 5.43 us -> none  [the longest x1 2.45 us: per_device(): jnp.dot(hidden, w_in, preferred_element_type=jnp.float32)]
    convert_element_type x3 -> x0, other arithmetic: 3.72 us -> none  [the longest x1 1.8 us: per_device(): partial_grad = lax.psum_scatter(flat_term.astype(jnp.bfloat16), 'dp', sca...]
    reduce_sum x5 -> x0, other arithmetic: 2.28 us -> none  [the longest x1 0.68 us: decode_terms(): jnp.sum(mask_rows.astype(jnp.float32))]
  transfers between devices with their start and end apart: 3 -> 0, of which waited for: 3 -> 0; matrix products, arithmetic and copies ran while one was open for 3% -> 0% of each run, Pallas kernels for 0% -> 0%
where the time goes in v1:
time: 31.1 us; the launch traced here: 30.9 us
  Pallas kernels  25.5 us (82%)
  local copies, waits for them, and re-layouts  3.14 us (10%)
  between operations  2.33 us (7%)
    pallas_call x1, Pallas kernels, per_device_kernel(): pl.pallas_call(functools.partial(kernel, (DP, T, S)), out_shape=(jax.Shap...  25.5 us
    unnamed x2, local copies, waits for them, and re-layouts  3.14 us

profile of v1, /device:TPU:0, one launch (start us, length us, event | category | flops | bytes accessed | tf_op | source)
XLA Modules:
  0.0 30.9 jit_solution(8582483821339989486)
XLA Ops:
  0.6 25.5 %decode.1 = (f32[1,1]{1,0:T(1,128)}, f32[128,128]{1,0:T(8,128)}, bf16[128,1024]{1,0:T(8,128)(2,1)}) custom-call(bf16[128,1024]{1,0:T(8,128)(2,1)} %hidden_h.1, bf16[1024,512]{1,0:T(8,128)(2,1)} %w_in_h.1, bf16[1024,512]{1,0:T(8,128)(2,1)} %embed_h.1, f32[1,512]{1,0:T(1,128)} %bitcast.7, bf16[512,1024]{1,0:T(8,128)(2,1)} %w_head_h.1, s32[8,128]{1,0:T(8,128)} %bitcast.6, ...), custom_call_target="tpu_custom_call" | custom-call | tf_op jit(solution)/shard_map/decode/pallas_call | solution.py:353
  26.7 1.5 %copy.14 = f32[16384]{0:T(1024)} copy(f32[16384]{0:T(1024)} %bitcast.5) | data formatting | bytes 131072
  28.1 1.7 %copy.15 = bf16[128,1024]{1,0:T(8,128)(2,1)} copy(bf16[128,1024]{1,0:T(8,128)(2,1)} %get-tuple-element.14) | data formatting | bytes 524288

commit v2 on v1

--- a/solution.py
+++ b/solution.py
@@ -92,8 +92,8 @@
     loss_o, head_o, gh_o,
     hidden, w_in, embed, gain, w_head, tokens, mask,
     ctx_own, ctx_send, ctx_recv, cnt, cnt_recv, gath, scaled, gl, hs, r1, s1, r2, s2, r3,
-    gc, gh, ls1, ls1_r, ls2, ls2_r, ls3, ls3_r,
-    in_sem, out_sem, ctx_ss, ctx_rs, cnt_ss, cnt_rs, gc_ss, gc_rs,
+    gc, ls1, ls1_r, ls2, ls2_r, ls3, ls3_r,
+    in_sem, ctx_ss, ctx_rs, cnt_ss, cnt_rs, gc_ss, gc_rs,
     h1_ss, h1_rs, h2_ss, h2_rs, h3_ss, h3_rs, l_ss, l_rs,
 ):
     DP, T, S = sizes
@@ -132,7 +132,11 @@
     for load in loads:
         load.start()
 
-    sends = []
+    sends, seen = [], set()
+
+    def got(copy):
+        copy.wait_recv()
+        seen.add(id(copy))
 
     def send(src, dst, ss, rs, peer):
         copy = pltpu.make_async_remote_copy(
@@ -180,7 +184,7 @@
 
     ctx = ctx_own[t]
     for d in range(1, T):
-        ctx_copies[d - 1].wait_recv()
+        got(ctx_copies[d - 1])
         ctx = ctx + ctx_recv[d - 1].astype(F32)
     ctx = ctx.astype(BF16).astype(F32)
     inputs = jnp.concatenate([ctx] * steps, 0) + jnp.concatenate(
@@ -241,7 +245,7 @@
     for j in range(DP):
         acc = hs[j, :, s].astype(F32)
         for e in range(1, S):
-            h1[j * (S - 1) + e - 1].wait_recv()
+            got(h1[j * (S - 1) + e - 1])
             acc = acc + r1[j, e - 1].astype(F32)
         s1[j] = acc.astype(BF16)
         for d in range(1, T):
@@ -251,7 +255,7 @@
             )
     lsum = ls1[...]
     for e in range(1, S):
-        lc1[e - 1].wait_recv()
+        got(lc1[e - 1])
         lsum = lsum + ls1_r[e - 1]
     ls2[...] = lsum
     lc2 = []
@@ -261,24 +265,22 @@
 
     total_mask = cnt[...]
     for i in range(len(peers_g)):
-        cnt_copies[i].wait_recv()
+        got(cnt_copies[i])
         total_mask = total_mask + cnt_recv[i]
     share = 1.0 / (total_mask[0:1, 0:1] * steps)
     for d in range(1, T):
-        gc_copies[d - 1].wait_recv()
+        got(gc_copies[d - 1])
     product = lax.dot_general(
         gc[...].reshape(nframes, width), w_in[...], (((1,), (1,)), ((), ())),
         preferred_element_type=F32,
     )
-    gh[...] = (product * share).astype(BF16)
-    out_copy = pltpu.make_async_copy(gh, gh_o, out_sem)
-    out_copy.start()
+    gh_o[...] = (product * share).astype(BF16)
 
     h3 = []
     for j in range(DP):
         acc = s1[j, t].astype(F32)
         for d in range(1, T):
-            h2[j * (T - 1) + d - 1].wait_recv()
+            got(h2[j * (T - 1) + d - 1])
             acc = acc + r2[j, d - 1].astype(F32)
         if j < DP - 1:
             s2[j] = acc.astype(BF16)
@@ -287,7 +289,7 @@
             )
     lsum = ls2[...]
     for d in range(1, T):
-        lc2[d - 1].wait_recv()
+        got(lc2[d - 1])
         lsum = lsum + ls2_r[d - 1]
     ls3[...] = lsum
     lc3 = []
@@ -297,19 +299,29 @@
         )
         n += 1
     for j in range(DP - 1):
-        h3[j].wait_recv()
+        got(h3[j])
         acc = acc + r3[j].astype(F32)
     acc = acc * share
     groups = vocab // 128
     for b in range(groups):
         head_o[pl.ds(b, piece, stride=groups), :] = acc[:, b * 128 : (b + 1) * 128]
     for d in range(1, DP):
-        lc3[d - 1].wait_recv()
+        got(lc3[d - 1])
         lsum = lsum + ls3_r[d - 1]
     loss_o[...] = lsum[0:1, 0:1] * share
-    out_copy.wait()
     for copy in sends:
         copy.wait_send()
+
+
+def write_out(loss_i, head_i, gh_i, loss_o, head_o, gh_o, sem):
+    copies = [
+        pltpu.make_async_copy(src, dst, sem.at[i])
+        for i, (src, dst) in enumerate([(gh_i, gh_o), (head_i, head_o), (loss_i, loss_o)])
+    ]
+    for copy in copies:
+        copy.start()
+    for copy in copies:
+        copy.wait()
 
 
 def per_device_kernel(hidden, w_in, embed, gain, w_head, tokens, frame_mask):
@@ -341,34 +353,40 @@
         V((DP - 1, piece, vocab), BF16),
         V((DP - 1, piece, vocab), BF16),
         V((T, frames, width), BF16),
-        V((nframes, feats), BF16),
         V((8, 128), F32), V((S - 1, 8, 128), F32),
         V((8, 128), F32), V((T - 1, 8, 128), F32),
         V((8, 128), F32), V((DP - 1, 8, 128), F32),
-        dma((7,)), dma,
+        dma((7,)),
         dma((T - 1,)), dma((T - 1,)), dma((G,)), dma((G,)), dma((T - 1,)), dma((T - 1,)),
         dma((DP, S - 1)), dma((DP, S - 1)), dma((DP, T - 1)), dma((DP, T - 1)),
         dma((DP - 1,)), dma((DP - 1,)), dma((S + T + DP - 3,)), dma((S + T + DP - 3,)),
     ]
-    loss, head, grad_hidden = pl.pallas_call(
+    shapes = (
+        jax.ShapeDtypeStruct((1, 1), F32),
+        jax.ShapeDtypeStruct((piece * vocab // 128, 128), F32),
+        jax.ShapeDtypeStruct((nframes, feats), BF16),
+    )
+    vmem = pl.BlockSpec(memory_space=pltpu.VMEM)
+    results = pl.pallas_call(
         functools.partial(kernel, (DP, T, S)),
-        out_shape=(
-            jax.ShapeDtypeStruct((1, 1), F32),
-            jax.ShapeDtypeStruct((piece * vocab // 128, 128), F32),
-            jax.ShapeDtypeStruct((nframes, feats), BF16),
-        ),
-        in_specs=[pl.BlockSpec(memory_space=pl.ANY)] * 7,
-        out_specs=(
-            pl.BlockSpec(memory_space=pltpu.VMEM),
-            pl.BlockSpec(memory_space=pltpu.VMEM),
-            pl.BlockSpec(memory_space=pl.ANY),
-        ),
+        out_shape=shapes,
+        in_specs=[pl.BlockSpec(memory_space=pltpu.HBM)] * 7,
+        out_specs=(vmem, vmem, vmem),
         scratch_shapes=scratch,
         compiler_params=pltpu.CompilerParams(
-            collective_id=0, has_side_effects=True, vmem_limit_bytes=63 << 20
+            collective_id=0, has_side_effects=True, vmem_limit_bytes=40 << 20
         ),
         name="decode",
-    )(hidden, w_in, embed, gain.reshape(1, -1), w_head, tokens.T, frame_mask.reshape(1, -1))
+    )(*[pltpu.with_memory_space_constraint(x, pltpu.HBM) for x in (hidden, w_in, embed, gain.reshape(1, -1), w_head, tokens.T, frame_mask.reshape(1, -1))])
+    loss, head, grad_hidden = pl.pallas_call(
+        write_out,
+        out_shape=shapes,
+        in_specs=[pl.BlockSpec(memory_space=pl.ANY)] * 3,
+        out_specs=(pl.BlockSpec(memory_space=pltpu.HBM),) * 3,
+        scratch_shapes=[dma((3,))],
+        compiler_params=pltpu.CompilerParams(vmem_limit_bytes=4 << 20),
+        name="write_out",
+    )(*results)
     return loss.reshape(()), head.reshape(-1), grad_hidden
 
 

time: 31.1 us -> 27.5 us (0.88)
  local copies, waits for them, and re-layouts: 3.14 us -> 0 us
  between operations: 2.33 us -> 0.64 us
  Pallas kernels: 25.5 us -> 26.7 us
    unnamed x2 -> x0, local copies, waits for them, and re-layouts: 3.14 us -> none
    pallas_call x1 -> x2, Pallas kernels: 25.5 us -> 26.7 us  [the longest x1 25.4 us: per_device_kernel(): pl.pallas_call(functools.partial(kernel, (DP, T, S)), out_shape=shapes, i...]
where the time goes in v2:
time: 27.5 us; the launch traced here: 27.4 us
  Pallas kernels  26.7 us (97%)
  between operations  0.64 us (2%)
    pallas_call x1, Pallas kernels, per_device_kernel(): pl.pallas_call(functools.partial(kernel, (DP, T, S)), out_shape=shapes, i...  25.4 us
    pallas_call x1, Pallas kernels, per_device_kernel(): pl.pallas_call(write_out, out_shape=shapes, in_specs=[pl.BlockSpec(memory...  1.38 us

profile of v2, /device:TPU:0, one launch (start us, length us, event | category | flops | bytes accessed | tf_op | source)
XLA Modules:
  0.0 27.4 jit_solution(14985815744193257028)
XLA Ops:
  0.6 25.4 %decode.1 = (f32[1,1]{1,0:T(1,128)}, f32[128,128]{1,0:T(8,128)S(1)}, bf16[128,1024]{1,0:T(8,128)(2,1)S(1)}) custom-call(bf16[128,1024]{1,0:T(8,128)(2,1)} %hidden_h.1, bf16[1024,512]{1,0:T(8,128)(2,1)} %w_in_h.1, bf16[1024,512]{1,0:T(8,128)(2,1)} %embed_h.1, f32[1,512]{1,0:T(1,128)} %bitcast.6, bf16[512,1024]{1,0:T(8,128)(2,1)} %w_head_h.1, ...), custom_call_target="tpu_custom_call" | custom-call | tf_op jit(solution)/shard_map/decode/pallas_call | solution.py:370
  26.0 1.4 %write_out.1 = (f32[1,1]{1,0:T(1,128)}, f32[128,128]{1,0:T(8,128)}, bf16[128,1024]{1,0:T(8,128)(2,1)}) custom-call(f32[1,1]{1,0:T(1,128)} %get-tuple-element.9.loss_i, f32[128,128]{1,0:T(8,128)S(1)} %get-tuple-element.10.head_i, bf16[128,1024]{1,0:T(8,128)(2,1)S(1)} %get-tuple-element.11.gh_i), custom_call_target="tpu_custom_call" | custom-call | tf_op jit(solution)/shard_map/write_out/pallas_call | solution.py:381

commit v3 on v2

--- a/solution.py
+++ b/solution.py
@@ -206,7 +206,12 @@
     gl[...] = grads
 
     chunk = width // DP
-    order = [lax.rem(a + 1 + j, DP) for j in range(DP)]
+    order = []
+    for j in range(DP - 1):
+        up = jnp.where(j < a, j, j + 1)
+        down = jnp.where(DP - 1 - j > a, DP - 1 - j, DP - 2 - j)
+        order.append(jnp.where(2 * a < DP, down, up))
+    order.append(a)
     h1 = []
     for j in range(DP):
         c = order[j]
@@ -226,20 +231,6 @@
     for e in range(1, S):
         lc1.append(send(ls1, ls1_r.at[e - 1], l_ss.at[n], l_rs.at[n], {"seq": lax.rem(s + e, S)}))
         n += 1
-
-    grad_scaled = lax.dot_general(
-        gl[...], w_head[...], (((1,), (1,)), ((), ())), preferred_element_type=F32
-    )
-    g = grad_scaled * gvec
-    gi = inverse * (g - normed * jnp.mean(g * normed, -1, keepdims=True))
-    gsum = gi[0:frames]
-    for k in range(1, steps):
-        gsum = gsum + gi[k * frames : (k + 1) * frames]
-    gc[t] = gsum.astype(BF16)
-    gc_copies = [
-        send(gc.at[t], gc.at[t], gc_ss.at[d - 1], gc_rs.at[d - 1], peers_t[d - 1])
-        for d in range(1, T)
-    ]
 
     h2 = []
     for j in range(DP):
@@ -263,6 +254,20 @@
         lc2.append(send(ls2, ls2_r.at[d - 1], l_ss.at[n], l_rs.at[n], peers_t[d - 1]))
         n += 1
 
+    grad_scaled = lax.dot_general(
+        gl[...], w_head[...], (((1,), (1,)), ((), ())), preferred_element_type=F32
+    )
+    g = grad_scaled * gvec
+    gi = inverse * (g - normed * jnp.mean(g * normed, -1, keepdims=True))
+    gsum = gi[0:frames]
+    for k in range(1, steps):
+        gsum = gsum + gi[k * frames : (k + 1) * frames]
+    gc[t] = gsum.astype(BF16)
+    gc_copies = [
+        send(gc.at[t], gc.at[t], gc_ss.at[d - 1], gc_rs.at[d - 1], peers_t[d - 1])
+        for d in range(1, T)
+    ]
+
     total_mask = cnt[...]
     for i in range(len(peers_g)):
         got(cnt_copies[i])
@@ -284,8 +289,9 @@
             acc = acc + r2[j, d - 1].astype(F32)
         if j < DP - 1:
             s2[j] = acc.astype(BF16)
+            slot = lax.rem(order[j] - a + DP, DP) - 1
             h3.append(
-                send(s2.at[j], r3.at[j], h3_ss.at[j], h3_rs.at[j], {"dp": order[j]})
+                send(s2.at[j], r3.at[slot], h3_ss.at[j], h3_rs.at[slot], {"dp": order[j]})
             )
     lsum = ls2[...]
     for d in range(1, T):
@@ -299,7 +305,11 @@
         )
         n += 1
     for j in range(DP - 1):
-        got(h3[j])
+        arrival = pltpu.make_async_remote_copy(
+            src_ref=s2.at[j], dst_ref=r3.at[j], send_sem=h3_ss.at[j], recv_sem=h3_rs.at[j],
+            device_id={"dp": lax.rem(a + 1, DP)}, device_id_type=MESH,
+        )
+        arrival.wait_recv()
         acc = acc + r3[j].astype(F32)
     acc = acc * share
     groups = vocab // 128

time: 27.5 us -> 29.7 us (1.080)
  Pallas kernels: 26.7 us -> 28.9 us
    pallas_call x1, Pallas kernels: 25.4 us -> 27.5 us  [per_device_kernel(): pl.pallas_call(functools.partial(kernel, (DP, T, S)), out_shape=shapes, i...]
where the time goes in v3:
time: 29.7 us; the launch traced here: 29.5 us
  Pallas kernels  28.9 us (97%)
  between operations  0.64 us (2%)
    pallas_call x1, Pallas kernels, per_device_kernel(): pl.pallas_call(functools.partial(kernel, (DP, T, S)), out_shape=shapes, i...  27.5 us
    pallas_call x1, Pallas kernels, per_device_kernel(): pl.pallas_call(write_out, out_shape=shapes, in_specs=[pl.BlockSpec(memory...  1.38 us

profile of v3, /device:TPU:0, one launch (start us, length us, event | category | flops | bytes accessed | tf_op | source)
XLA Modules:
  0.0 29.5 jit_solution(3716034346729277118)
XLA Ops:
  0.6 27.5 %decode.1 = (f32[1,1]{1,0:T(1,128)}, f32[128,128]{1,0:T(8,128)S(1)}, bf16[128,1024]{1,0:T(8,128)(2,1)S(1)}) custom-call(bf16[128,1024]{1,0:T(8,128)(2,1)} %hidden_h.1, bf16[1024,512]{1,0:T(8,128)(2,1)} %w_in_h.1, bf16[1024,512]{1,0:T(8,128)(2,1)} %embed_h.1, f32[1,512]{1,0:T(1,128)} %bitcast.6, bf16[512,1024]{1,0:T(8,128)(2,1)} %w_head_h.1, ...), custom_call_target="tpu_custom_call" | custom-call | tf_op jit(solution)/shard_map/decode/pallas_call | solution.py:380
  28.2 1.4 %write_out.1 = (f32[1,1]{1,0:T(1,128)}, f32[128,128]{1,0:T(8,128)}, bf16[128,1024]{1,0:T(8,128)(2,1)}) custom-call(f32[1,1]{1,0:T(1,128)} %get-tuple-element.9.loss_i, f32[128,128]{1,0:T(8,128)S(1)} %get-tuple-element.10.head_i, bf16[128,1024]{1,0:T(8,128)(2,1)S(1)} %get-tuple-element.11.gh_i), custom_call_target="tpu_custom_call" | custom-call | tf_op jit(solution)/shard_map/write_out/pallas_call | solution.py:391

commit v4 on v3

--- a/solution.py
+++ b/solution.py
@@ -268,19 +268,6 @@
         for d in range(1, T)
     ]
 
-    total_mask = cnt[...]
-    for i in range(len(peers_g)):
-        got(cnt_copies[i])
-        total_mask = total_mask + cnt_recv[i]
-    share = 1.0 / (total_mask[0:1, 0:1] * steps)
-    for d in range(1, T):
-        got(gc_copies[d - 1])
-    product = lax.dot_general(
-        gc[...].reshape(nframes, width), w_in[...], (((1,), (1,)), ((), ())),
-        preferred_element_type=F32,
-    )
-    gh_o[...] = (product * share).astype(BF16)
-
     h3 = []
     for j in range(DP):
         acc = s1[j, t].astype(F32)
@@ -304,6 +291,19 @@
             send(ls3, ls3_r.at[d - 1], l_ss.at[n], l_rs.at[n], {"dp": lax.rem(a + d, DP)})
         )
         n += 1
+    total_mask = cnt[...]
+    for i in range(len(peers_g)):
+        got(cnt_copies[i])
+        total_mask = total_mask + cnt_recv[i]
+    share = 1.0 / (total_mask[0:1, 0:1] * steps)
+    for d in range(1, T):
+        got(gc_copies[d - 1])
+    product = lax.dot_general(
+        gc[...].reshape(nframes, width), w_in[...], (((1,), (1,)), ((), ())),
+        preferred_element_type=F32,
+    )
+    gh_o[...] = (product * share).astype(BF16)
+
     for j in range(DP - 1):
         arrival = pltpu.make_async_remote_copy(
             src_ref=s2.at[j], dst_ref=r3.at[j], send_sem=h3_ss.at[j], recv_sem=h3_rs.at[j],

time: 29.7 us -> 26.9 us (0.906)
  Pallas kernels: 28.9 us -> 26.1 us
    pallas_call x1, Pallas kernels: 27.5 us -> 24.8 us  [per_device_kernel(): pl.pallas_call(functools.partial(kernel, (DP, T, S)), out_shape=shapes, i...]
where the time goes in v4:
time: 26.9 us; the launch traced here: 26.8 us
  Pallas kernels  26.1 us (97%)
  between operations  0.64 us (2%)
    pallas_call x1, Pallas kernels, per_device_kernel(): pl.pallas_call(functools.partial(kernel, (DP, T, S)), out_shape=shapes, i...  24.8 us
    pallas_call x1, Pallas kernels, per_device_kernel(): pl.pallas_call(write_out, out_shape=shapes, in_specs=[pl.BlockSpec(memory...  1.38 us

profile of v4, /device:TPU:0, one launch (start us, length us, event | category | flops | bytes accessed | tf_op | source)
XLA Modules:
  0.0 26.8 jit_solution(2058200142582578333)
XLA Ops:
  0.6 24.8 %decode.1 = (f32[1,1]{1,0:T(1,128)}, f32[128,128]{1,0:T(8,128)S(1)}, bf16[128,1024]{1,0:T(8,128)(2,1)S(1)}) custom-call(bf16[128,1024]{1,0:T(8,128)(2,1)} %hidden_h.1, bf16[1024,512]{1,0:T(8,128)(2,1)} %w_in_h.1, bf16[1024,512]{1,0:T(8,128)(2,1)} %embed_h.1, f32[1,512]{1,0:T(1,128)} %bitcast.6, bf16[512,1024]{1,0:T(8,128)(2,1)} %w_head_h.1, ...), custom_call_target="tpu_custom_call" | custom-call | tf_op jit(solution)/shard_map/decode/pallas_call | solution.py:380
  25.4 1.4 %write_out.1 = (f32[1,1]{1,0:T(1,128)}, f32[128,128]{1,0:T(8,128)}, bf16[128,1024]{1,0:T(8,128)(2,1)}) custom-call(f32[1,1]{1,0:T(1,128)} %get-tuple-element.9.loss_i, f32[128,128]{1,0:T(8,128)S(1)} %get-tuple-element.10.head_i, bf16[128,1024]{1,0:T(8,128)(2,1)S(1)} %get-tuple-element.11.gh_i), custom_call_target="tpu_custom_call" | custom-call | tf_op jit(solution)/shard_map/write_out/pallas_call | solution.py:391

commit v5 on v4

--- a/solution.py
+++ b/solution.py
@@ -212,28 +212,9 @@
         down = jnp.where(DP - 1 - j > a, DP - 1 - j, DP - 2 - j)
         order.append(jnp.where(2 * a < DP, down, up))
     order.append(a)
-    h1 = []
-    for j in range(DP):
-        c = order[j]
-        cols = scaled[:, pl.ds(pl.multiple_of(c * chunk, chunk), chunk)]
-        term = lax.dot_general(
-            cols, gl[...], (((0,), (0,)), ((), ())), preferred_element_type=F32
-        )
-        hs[j] = term.astype(BF16).reshape(T, S, piece, vocab)
-        for e in range(1, S):
-            h1.append(
-                send(hs.at[j, :, lax.rem(s + e, S)], r1.at[j, e - 1], h1_ss.at[j, e - 1],
-                     h1_rs.at[j, e - 1], {"seq": lax.rem(s + e, S)})
-            )
-    ls1[...] = jnp.zeros(ls1.shape, F32) + jnp.sum(weights * nll)
-    n = 0
-    lc1 = []
-    for e in range(1, S):
-        lc1.append(send(ls1, ls1_r.at[e - 1], l_ss.at[n], l_rs.at[n], {"seq": lax.rem(s + e, S)}))
-        n += 1
-
-    h2 = []
-    for j in range(DP):
+    h1, h2 = [], []
+
+    def tensor_stage(j):
         acc = hs[j, :, s].astype(F32)
         for e in range(1, S):
             got(h1[j * (S - 1) + e - 1])
@@ -244,6 +225,31 @@
                 send(s1.at[j, lax.rem(t + d, T)], r2.at[j, d - 1], h2_ss.at[j, d - 1],
                      h2_rs.at[j, d - 1], peers_t[d - 1])
             )
+
+    lag = 2
+    for j in range(DP):
+        c = order[j]
+        cols = scaled[:, pl.ds(pl.multiple_of(c * chunk, chunk), chunk)]
+        term = lax.dot_general(
+            cols, gl[...], (((0,), (0,)), ((), ())), preferred_element_type=F32
+        )
+        hs[j] = term.astype(BF16).reshape(T, S, piece, vocab)
+        for e in range(1, S):
+            h1.append(
+                send(hs.at[j, :, lax.rem(s + e, S)], r1.at[j, e - 1], h1_ss.at[j, e - 1],
+                     h1_rs.at[j, e - 1], {"seq": lax.rem(s + e, S)})
+            )
+        if j >= lag:
+            tensor_stage(j - lag)
+    for j in range(max(DP - lag, 0), DP):
+        tensor_stage(j)
+    ls1[...] = jnp.zeros(ls1.shape, F32) + jnp.sum(weights * nll)
+    n = 0
+    lc1 = []
+    for e in range(1, S):
+        lc1.append(send(ls1, ls1_r.at[e - 1], l_ss.at[n], l_rs.at[n], {"seq": lax.rem(s + e, S)}))
+        n += 1
+
     lsum = ls1[...]
     for e in range(1, S):
         got(lc1[e - 1])

time: 26.9 us -> 26.6 us (0.989)
  Pallas kernels: 26.1 us -> 25.8 us
    pallas_call x1, Pallas kernels: 24.8 us -> 24.4 us  [per_device_kernel(): pl.pallas_call(functools.partial(kernel, (DP, T, S)), out_shape=shapes, i...]
where the time goes in v5:
time: 26.6 us; the launch traced here: 26.4 us
  Pallas kernels  25.8 us (97%)
  between operations  0.64 us (2%)
    pallas_call x1, Pallas kernels, per_device_kernel(): pl.pallas_call(functools.partial(kernel, (DP, T, S)), out_shape=shapes, i...  24.4 us
    pallas_call x1, Pallas kernels, per_device_kernel(): pl.pallas_call(write_out, out_shape=shapes, in_specs=[pl.BlockSpec(memory...  1.38 us

profile of v5, /device:TPU:0, one launch (start us, length us, event | category | flops | bytes accessed | tf_op | source)
XLA Modules:
  0.0 26.4 jit_solution(8074363447877348608)
XLA Ops:
  0.6 24.4 %decode.1 = (f32[1,1]{1,0:T(1,128)}, f32[128,128]{1,0:T(8,128)S(1)}, bf16[128,1024]{1,0:T(8,128)(2,1)S(1)}) custom-call(bf16[128,1024]{1,0:T(8,128)(2,1)} %hidden_h.1, bf16[1024,512]{1,0:T(8,128)(2,1)} %w_in_h.1, bf16[1024,512]{1,0:T(8,128)(2,1)} %embed_h.1, f32[1,512]{1,0:T(1,128)} %bitcast.6, bf16[512,1024]{1,0:T(8,128)(2,1)} %w_head_h.1, ...), custom_call_target="tpu_custom_call" | custom-call | tf_op jit(solution)/shard_map/decode/pallas_call | solution.py:386
  25.0 1.4 %write_out.1 = (f32[1,1]{1,0:T(1,128)}, f32[128,128]{1,0:T(8,128)}, bf16[128,1024]{1,0:T(8,128)(2,1)}) custom-call(f32[1,1]{1,0:T(1,128)} %get-tuple-element.9.loss_i, f32[128,128]{1,0:T(8,128)S(1)} %get-tuple-element.10.head_i, bf16[128,1024]{1,0:T(8,128)(2,1)S(1)} %get-tuple-element.11.gh_i), custom_call_target="tpu_custom_call" | custom-call | tf_op jit(solution)/shard_map/write_out/pallas_call | solution.py:397

commit v6 on v5

--- a/solution.py
+++ b/solution.py
@@ -206,12 +206,7 @@
     gl[...] = grads
 
     chunk = width // DP
-    order = []
-    for j in range(DP - 1):
-        up = jnp.where(j < a, j, j + 1)
-        down = jnp.where(DP - 1 - j > a, DP - 1 - j, DP - 2 - j)
-        order.append(jnp.where(2 * a < DP, down, up))
-    order.append(a)
+    order = [lax.rem(a + 1 + j, DP) for j in range(DP)]
     h1, h2 = [], []
 
     def tensor_stage(j):

time: 26.6 us -> 26.6 us (level)
  no operation moved by 1% of the time
where the time goes in v6:
time: 26.6 us; the launch traced here: 26.4 us
  Pallas kernels  25.8 us (97%)
  between operations  0.64 us (2%)
    pallas_call x1, Pallas kernels, per_device_kernel(): pl.pallas_call(functools.partial(kernel, (DP, T, S)), out_shape=shapes, i...  24.4 us
    pallas_call x1, Pallas kernels, per_device_kernel(): pl.pallas_call(write_out, out_shape=shapes, in_specs=[pl.BlockSpec(memory...  1.38 us

profile of v6, /device:TPU:0, one launch (start us, length us, event | category | flops | bytes accessed | tf_op | source)
XLA Modules:
  0.0 26.4 jit_solution(2600740840765773277)
XLA Ops:
  0.6 24.4 %decode.1 = (f32[1,1]{1,0:T(1,128)}, f32[128,128]{1,0:T(8,128)S(1)}, bf16[128,1024]{1,0:T(8,128)(2,1)S(1)}) custom-call(bf16[128,1024]{1,0:T(8,128)(2,1)} %hidden_h.1, bf16[1024,512]{1,0:T(8,128)(2,1)} %w_in_h.1, bf16[1024,512]{1,0:T(8,128)(2,1)} %embed_h.1, f32[1,512]{1,0:T(1,128)} %bitcast.6, bf16[512,1024]{1,0:T(8,128)(2,1)} %w_head_h.1, ...), custom_call_target="tpu_custom_call" | custom-call | tf_op jit(solution)/shard_map/decode/pallas_call | solution.py:381
  25.0 1.4 %write_out.1 = (f32[1,1]{1,0:T(1,128)}, f32[128,128]{1,0:T(8,128)}, bf16[128,1024]{1,0:T(8,128)(2,1)}) custom-call(f32[1,1]{1,0:T(1,128)} %get-tuple-element.9.loss_i, f32[128,128]{1,0:T(8,128)S(1)} %get-tuple-element.10.head_i, bf16[128,1024]{1,0:T(8,128)(2,1)S(1)} %get-tuple-element.11.gh_i), custom_call_target="tpu_custom_call" | custom-call | tf_op jit(solution)/shard_map/write_out/pallas_call | solution.py:392

commit v7 on v5

--- a/solution.py
+++ b/solution.py
@@ -226,7 +226,7 @@
                      h2_rs.at[j, d - 1], peers_t[d - 1])
             )
 
-    lag = 2
+    lag = 1
     for j in range(DP):
         c = order[j]
         cols = scaled[:, pl.ds(pl.multiple_of(c * chunk, chunk), chunk)]

time: 26.6 us -> 26 us (0.977)
  Pallas kernels: 25.8 us -> 25.2 us
    pallas_call x1, Pallas kernels: 24.4 us -> 23.9 us  [per_device_kernel(): pl.pallas_call(functools.partial(kernel, (DP, T, S)), out_shape=shapes, i...]
where the time goes in v7:
time: 26 us; the launch traced here: 25.9 us
  Pallas kernels  25.2 us (97%)
  between operations  0.64 us (2%)
    pallas_call x1, Pallas kernels, per_device_kernel(): pl.pallas_call(functools.partial(kernel, (DP, T, S)), out_shape=shapes, i...  23.9 us
    pallas_call x1, Pallas kernels, per_device_kernel(): pl.pallas_call(write_out, out_shape=shapes, in_specs=[pl.BlockSpec(memory...  1.38 us

profile of v7, /device:TPU:0, one launch (start us, length us, event | category | flops | bytes accessed | tf_op | source)
XLA Modules:
  0.0 25.9 jit_solution(1636471244529271298)
XLA Ops:
  0.6 23.9 %decode.1 = (f32[1,1]{1,0:T(1,128)}, f32[128,128]{1,0:T(8,128)S(1)}, bf16[128,1024]{1,0:T(8,128)(2,1)S(1)}) custom-call(bf16[128,1024]{1,0:T(8,128)(2,1)} %hidden_h.1, bf16[1024,512]{1,0:T(8,128)(2,1)} %w_in_h.1, bf16[1024,512]{1,0:T(8,128)(2,1)} %embed_h.1, f32[1,512]{1,0:T(1,128)} %bitcast.6, bf16[512,1024]{1,0:T(8,128)(2,1)} %w_head_h.1, ...), custom_call_target="tpu_custom_call" | custom-call | tf_op jit(solution)/shard_map/decode/pallas_call | solution.py:386
  24.5 1.4 %write_out.1 = (f32[1,1]{1,0:T(1,128)}, f32[128,128]{1,0:T(8,128)}, bf16[128,1024]{1,0:T(8,128)(2,1)}) custom-call(f32[1,1]{1,0:T(1,128)} %get-tuple-element.9.loss_i, f32[128,128]{1,0:T(8,128)S(1)} %get-tuple-element.10.head_i, bf16[128,1024]{1,0:T(8,128)(2,1)S(1)} %get-tuple-element.11.gh_i), custom_call_target="tpu_custom_call" | custom-call | tf_op jit(solution)/shard_map/write_out/pallas_call | solution.py:397
